TPU v7x, 32 devices: a whole 2x2x4 slice. The times are simulated.
32 devices in a mesh: dp: 4 (over x, core), expert: 8 (over z, y).
Axes of the slice: x: 2, y: 2, z: 4, core: 2. Of those that a mesh axis runs over, the one named last changes fastest.
Arguments:
- tokens: bfloat16 [4096, 4096], P(('dp', 'expert')), may hold values from -6 to 6
- expert_ids: int32 [4096, 2], P(('dp', 'expert')), may hold values from 0 to 7, as said below
- gate_codes: int32 [4096, 2], P(('dp', 'expert')), may hold values from 1 to 64
- w_gate: bfloat16 [8, 4096, 768], P('expert'), may hold values from -0.09375 to 0.09375
- w_up: bfloat16 [8, 4096, 768], P('expert'), may hold values from -0.09375 to 0.09375
- w_down: bfloat16 [8, 768, 4096], P('expert'), may hold values from -0.21875 to 0.21875
- out_grad: bfloat16 [4096, 4096], P(('dp', 'expert')), may hold values from -6 to 6
Outputs:
- layer_out: bfloat16 [4096, 4096], P(('dp', 'expert'))
- tokens_grad: bfloat16 [4096, 4096], P(('dp', 'expert'))
- gate_weight_grad: bfloat16 [8, 4096, 768], P('expert', 'dp')
- up_weight_grad: bfloat16 [8, 4096, 768], P('expert', 'dp')
- down_weight_grad: bfloat16 [8, 768, 4096], P('expert', None, 'dp')
Inputs may be any that keep to these rules, and one draw needn't show every extreme that they name: `expert_ids`: each token names 2 different experts. In the rows of one device no expert is named more than 48 times, and in every draw one and the same expert is named exactly 48 times by the rows of every device.
All inputs are finite; a program needn't handle non-finite values.
Results may differ from a plain program's by a relative error of at most 0.009.
Values may be sent and summed in bfloat16 or wider, within the bound.
A program may use at most 192 MiB of HBM per device.

v0:
```python
import jax
import jax.numpy as jnp
from jax import lax
from jax.sharding import PartitionSpec as P


def slot_targets(block_ids, experts, capacity):
    flat_ids = block_ids.reshape(-1)
    one_hot = (flat_ids[:, None] == jnp.arange(experts, dtype=jnp.int32)[None, :]).astype(jnp.int32)
    earlier = jnp.cumsum(one_hot, axis=0) - one_hot
    slot_ranks = jnp.sum(earlier * one_hot, axis=1)
    return flat_ids * capacity + slot_ranks


def per_device(tokens, expert_ids, gate_codes, w_gate, w_up, w_down, out_grad):
    experts = lax.axis_size("expert")
    tok_count, model_width = tokens.shape
    top_count = expert_ids.shape[1]
    pair_count = tok_count * top_count
    capacity = 3 * pair_count // (2 * experts)
    targets = slot_targets(expert_ids, experts, capacity)
    owners = (
        jnp.full((experts * capacity,), -1, jnp.int32)
        .at[targets]
        .set(jnp.arange(pair_count, dtype=jnp.int32))
    )
    is_live = owners >= 0
    safe_pair = jnp.maximum(owners, 0)
    token_pos = safe_pair // top_count
    gate_flat = gate_codes.astype(jnp.float32).reshape(-1) / 64.0
    pair_gains = jnp.where(is_live, gate_flat[safe_pair], 0.0)
    outbound = jnp.where(is_live[:, None], tokens[token_pos], jnp.zeros((), jnp.bfloat16))
    outbound = outbound.reshape(experts, capacity, model_width)
    gate_matrix = w_gate[0]
    up_matrix = w_up[0]
    down_matrix = w_down[0]
    hidden_units = gate_matrix.shape[1]
    contract = (((1,), (1,)), ((), ()))
    contract_rows = (((0,), (0,)), ((), ()))
    received = lax.all_to_all(outbound, "expert", split_axis=0, concat_axis=0, tiled=True)
    slot_count = received.shape[1]
    expert_row_block = received.reshape(-1, model_width)
    pre_gate = jnp.dot(expert_row_block, gate_matrix, preferred_element_type=jnp.float32)
    pre_up = jnp.dot(expert_row_block, up_matrix, preferred_element_type=jnp.float32)
    expert_hidden = (pre_gate * jax.nn.sigmoid(pre_gate) * pre_up).astype(jnp.bfloat16)
    produced = jnp.dot(expert_hidden, down_matrix, preferred_element_type=jnp.float32).astype(
        jnp.bfloat16
    )
    produced = produced.reshape(experts, slot_count, model_width)
    returned = lax.all_to_all(produced, "expert", split_axis=0, concat_axis=0, tiled=True)
    returned, arrived, pre_gate, pre_up, hidden = (
        returned,
        received,
        pre_gate.reshape(experts, slot_count, hidden_units),
        pre_up.reshape(experts, slot_count, hidden_units),
        expert_hidden.reshape(experts, slot_count, hidden_units),
    )
    pair_out = returned.reshape(-1, model_width)[targets].astype(jnp.float32)
    weighted = gate_flat[:, None] * pair_out
    layer_out = jnp.sum(weighted.reshape(tok_count, top_count, model_width), axis=1).astype(
        jnp.bfloat16
    )
    upstream = out_grad[token_pos]
    pair_grad = (pair_gains[:, None] * upstream.astype(jnp.float32)).astype(jnp.bfloat16)
    pair_grad = pair_grad.reshape(experts, capacity, model_width)
    incoming = lax.all_to_all(pair_grad, "expert", split_axis=0, concat_axis=0, tiled=True).reshape(
        -1, model_width
    )
    pre_gate = pre_gate.reshape(-1, hidden_units)
    pre_up = pre_up.reshape(-1, hidden_units)
    hidden = hidden.reshape(-1, hidden_units)
    sigmoid_gate = jax.nn.sigmoid(pre_gate)
    silu_gate = pre_gate * sigmoid_gate
    hidden_grad = lax.dot_general(
        incoming, down_matrix, contract, preferred_element_type=jnp.float32
    )
    gate_pre_grad = (
        hidden_grad * pre_up * sigmoid_gate * (1.0 + pre_gate * (1.0 - sigmoid_gate))
    ).astype(jnp.bfloat16)
    up_pre_grad = (hidden_grad * silu_gate).astype(jnp.bfloat16)
    input_grad = lax.dot_general(
        gate_pre_grad, gate_matrix, contract, preferred_element_type=jnp.float32
    )
    input_grad = input_grad + lax.dot_general(
        up_pre_grad, up_matrix, contract, preferred_element_type=jnp.float32
    )
    input_grad = input_grad.astype(jnp.bfloat16).reshape(experts, capacity, model_width)
    returned_grad = lax.all_to_all(input_grad, "expert", split_axis=0, concat_axis=0, tiled=True)
    pair_input = returned_grad.reshape(-1, model_width)[targets].astype(jnp.float32)
    tokens_grad = jnp.sum(pair_input.reshape(tok_count, top_count, model_width), axis=1).astype(
        jnp.bfloat16
    )
    row_block = arrived.reshape(-1, model_width)
    column_block = row_block
    gate_sum = lax.psum_scatter(
        lax.dot_general(
            column_block, gate_pre_grad, contract_rows, preferred_element_type=jnp.float32
        ).astype(jnp.bfloat16),
        "dp",
        scatter_dimension=0,
        tiled=True,
    )
    column_block = row_block
    up_sum = lax.psum_scatter(
        lax.dot_general(
            column_block, up_pre_grad, contract_rows, preferred_element_type=jnp.float32
        ).astype(jnp.bfloat16),
        "dp",
        scatter_dimension=0,
        tiled=True,
    )
    column_block = incoming
    down_sum = (
        lax.psum_scatter(
            lax.dot_general(
                column_block, hidden, contract_rows, preferred_element_type=jnp.float32
            ).astype(jnp.bfloat16),
            "dp",
            scatter_dimension=0,
            tiled=True,
        )
        .astype(jnp.float32)
        .T
    )
    return (
        layer_out,
        tokens_grad,
        gate_sum[None],
        up_sum[None],
        down_sum.astype(jnp.bfloat16)[None],
    )


def solution(mesh):
    placed = (
        P(("dp", "expert"), None),
        P(("dp", "expert"), None),
        P(("dp", "expert"), None),
        P("expert", None, None),
        P("expert", None, None),
        P("expert", None, None),
        P(("dp", "expert"), None),
    )
    return jax.shard_map(
        per_device,
        mesh=mesh,
        in_specs=placed,
        out_specs=(
            P(("dp", "expert"), None),
            P(("dp", "expert"), None),
            P("expert", "dp", None),
            P("expert", "dp", None),
            P("expert", None, "dp"),
        ),
        check_vma=False,
    )
```

profile of v0, /device:TPU:0, one launch (start us, length us, event | category | flops | bytes accessed | tf_op | source)
XLA Modules:
  0.0 404.6 jit_solution(15272280271444568787)
XLA Ops:
  7.2 0.8 broadcast_multiply_fusion
  8.0 0.8 copy.16
  8.7 0.1 eq.29
  8.9 0.1 eq.25
  9.0 0.7 convert_multiply_fusion.1
  9.7 0.1 copy.14
  9.8 0.1 div.22
  10.0 0.1 copy.15
  10.1 0.1 mul.64
  10.2 0.6 reduce-window.6
  10.8 0.2 slice_reduce_fusion
  11.1 0.1 fusion.20
  11.2 1.4 scatter_custom_fusion
  12.6 2.8 gather_fusion.2
  15.5 0.1 mul.69
  15.5 4.1 %gather_fusion.3 = bf16[384,4096]{1,0:T(8,128)(2,1)} fusion(bf16[128,4096]{1,0:T(8,128)(2,1)S(1)} %copy-done, s32[1024]{0:T(1024)S(1)} %get-tuple-element.23), kind=kCustom, calls=%fused_computation.3 | custom fusion | bytes 6292992 | tf_op jit(solution)/shard_map/gather | solution.py:63
  19.6 4.6 %fusion = bf16[8,48,4096]{2,1,0:T(8,128)(2,1)} fusion(bf16[8,48,4096]{2,1,0:T(8,128)(2,1)} %bitcast.60, f32[8,48]{1,0:T(8,128)S(1)} %mul.69), kind=kLoop, calls=%fused_computation.10 | loop fusion | flops 4718592 | bytes 6292992 | tf_op jit(solution)/shard_map/convert_element_type | solution.py:64
  24.2 7.4 %all-to-all-start.2 = ((bf16[8,48,4096]{2,1,0:T(8,128)(2,1)}), bf16[8,48,4096]{2,1,0:T(8,128)(2,1)}, u32[]{:S(2)}, u32[]{:S(2)}) async-start(bf16[8,48,4096]{2,1,0:T(8,128)(2,1)} %fusion), calls=%async_computation.2 | async-start | bytes 6291456 | tf_op jit(solution)/shard_map/all_to_all | solution.py:66
  31.6 0.1 broadcast_in_dim.45
  31.7 4.0 gather_fusion
  35.7 3.9 broadcast_select_fusion
  39.6 62.8 %all-to-all-done.2 = bf16[8,48,4096]{2,1,0:T(8,128)(2,1)} async-done(((bf16[8,48,4096]{2,1,0:T(8,128)(2,1)}), bf16[8,48,4096]{2,1,0:T(8,128)(2,1)}, u32[]{:S(2)}, u32[]{:S(2)}) %all-to-all-start.2) | async-done | bytes 3145760 | tf_op jit(solution)/shard_map/all_to_all | solution.py:66
  102.4 3.6 all-to-all-start
  106.1 0.5 reduce-scatter.8.cloned.1.call-start
  106.6 7.4 %fusion.1 = f32[384,768]{1,0:T(8,128)} fusion(bf16[384,4096]{1,0:T(8,128)(2,1)} %bitcast.12, bf16[1,768,4096]{2,1,0:T(8,128)(2,1)} %param.12), kind=kOutput, calls=%fused_computation.11 | convolution fusion | flops 2415919104 | bytes 10616832 | tf_op jit(solution)/shard_map/dot_general | solution.py:74
  114.0 63.0 %all-to-all-done = bf16[8,48,4096]{2,1,0:T(8,128)(2,1)S(1)} async-done(((bf16[8,48,4096]{2,1,0:T(8,128)(2,1)}), bf16[8,48,4096]{2,1,0:T(8,128)(2,1)S(1)}, u32[]{:S(2)}, u32[]{:S(2)}) %all-to-all-start) | async-done | bytes 3145760 | tf_op jit(solution)/shard_map/all_to_all | solution.py:40
  176.9 5.5 %fusion.7 = f32[384,768]{1,0:T(8,128)S(1)} fusion(bf16[384,4096]{1,0:T(8,128)(2,1)S(1)} %bitcast.61, bf16[1,4096,768]{2,1,0:T(8,128)(2,1)} %param.11), kind=kOutput, calls=%fused_computation.17 | convolution fusion | flops 2415919104 | bytes 10616832 | tf_op jit(solution)/shard_map/dot_general | solution.py:44
  182.4 6.8 %multiply_convert_fusion.1 = (bf16[384,768]{1,0:T(8,128)(2,1)}, bf16[384,768]{1,0:T(8,128)(2,1)}, bf16[384,768]{1,0:T(8,128)(2,1)S(1)}) fusion(f32[384,768]{1,0:T(8,128)S(1)} %copy-done.6, f32[384,768]{1,0:T(8,128)S(1)} %fusion.7, bf16[384,4096]{1,0:T(8,128)(2,1)S(1)} %bitcast.62, bf16[1,4096,768]{2,1,0:T(8,128)(2,1)} %param.10), kind=kOutput, calls=%fused_computation.28 | convolution fusion | flops 2420342784 | bytes 13565952 | tf_op jit(solution)/shard_map/dot_general | solution.py:43
  189.2 0.8 copy-done.4
  190.0 8.0 %convolution_convert_fusion = bf16[4096,768]{1,0:T(8,128)(2,1)} fusion(bf16[384,4096]{1,0:T(8,128)(2,1)} %bitcast.12, bf16[384,768]{1,0:T(8,128)(2,1)S(1)} %get-tuple-element.19), kind=kOutput, calls=%fused_computation.6 | convolution fusion | flops 2419064832 | bytes 10027008 | tf_op jit(solution)/shard_map/dot_general | solution.py:115
  198.1 6.4 %convolution_convert_fusion.2 = bf16[4096,768]{1,0:T(8,128)(2,1)} fusion(bf16[384,4096]{1,0:T(8,128)(2,1)S(1)} %bitcast.63, bf16[384,768]{1,0:T(8,128)(2,1)} %get-tuple-element.17), kind=kOutput, calls=%fused_computation.8 | convolution fusion | flops 2419064832 | bytes 10027008 | tf_op jit(solution)/shard_map/dot_general | solution.py:96
  204.6 0.2 reduce-scatter.6.cloned.1.call-start
  204.8 6.7 %convolution_convert_fusion.1 = bf16[4096,768]{1,0:T(8,128)(2,1)} fusion(bf16[384,4096]{1,0:T(8,128)(2,1)S(1)} %bitcast.64, bf16[384,768]{1,0:T(8,128)(2,1)} %get-tuple-element.18), kind=kOutput, calls=%fused_computation.7 | convolution fusion | flops 2419064832 | bytes 10027008 | tf_op jit(solution)/shard_map/dot_general | solution.py:105
  211.5 1.0 copy-done.5
  212.5 6.8 %fusion.15 = bf16[384,4096]{1,0:T(8,128)(2,1)} fusion(bf16[384,768]{1,0:T(8,128)(2,1)S(1)} %copy-done.5, bf16[1,768,4096]{2,1,0:T(8,128)(2,1)} %param.12), kind=kOutput, calls=%fused_computation.24 | convolution fusion | flops 2417491968 | bytes 10027008 | tf_op jit(solution)/shard_map/dot_general | solution.py:46
  219.3 3.7 all-to-all-start.1
  223.0 4.9 %fusion.5 = f32[384,4096]{1,0:T(8,128)S(1)} fusion(bf16[384,768]{1,0:T(8,128)(2,1)} %get-tuple-element.18, bf16[1,4096,768]{2,1,0:T(8,128)(2,1)} %param.11), kind=kOutput, calls=%fused_computation.15 | convolution fusion | flops 2415919104 | bytes 13172736 | tf_op jit(solution)/shard_map/dot_general | solution.py:84
  227.9 8.5 %add_convert_fusion = bf16[384,4096]{1,0:T(8,128)(2,1)} fusion(f32[384,4096]{1,0:T(8,128)S(1)} %fusion.5, bf16[384,768]{1,0:T(8,128)(2,1)S(1)} %copy-done.3, bf16[1,4096,768]{2,1,0:T(8,128)(2,1)} %param.10), kind=kOutput, calls=%fused_computation.23 | convolution fusion | flops 2419064832 | bytes 16318464 | tf_op jit(solution)/shard_map/dot_general | solution.py:81
  236.5 57.5 %all-to-all-done.1 = bf16[8,48,4096]{2,1,0:T(8,128)(2,1)S(1)} async-done(((bf16[8,48,4096]{2,1,0:T(8,128)(2,1)}), bf16[8,48,4096]{2,1,0:T(8,128)(2,1)S(1)}, u32[]{:S(2)}, u32[]{:S(2)}) %all-to-all-start.1) | async-done | bytes 3145760 | tf_op jit(solution)/shard_map/all_to_all | solution.py:50
  294.0 4.4 %all-to-all-start.3 = ((bf16[8,48,4096]{2,1,0:T(8,128)(2,1)}), bf16[8,48,4096]{2,1,0:T(8,128)(2,1)}, u32[]{:S(2)}, u32[]{:S(2)}) async-start(bf16[8,48,4096]{2,1,0:T(8,128)(2,1)} %bitcast.65), calls=%async_computation.3 | async-start | bytes 6291456 | tf_op jit(solution)/shard_map/all_to_all | solution.py:88
  298.4 3.2 gather_fusion.1
  301.6 5.5 %reshape.118 = f32[128,2,4096]{2,1,0:T(2,128)} reshape(bf16[256,4096]{1,0:T(8,128)(2,1)} %gather_fusion.1) | data formatting | bytes 6291456 | tf_op jit(solution)/shard_map/convert_element_type | solution.py:58
  307.1 61.5 %all-to-all-done.3 = bf16[8,48,4096]{2,1,0:T(8,128)(2,1)} async-done(((bf16[8,48,4096]{2,1,0:T(8,128)(2,1)}), bf16[8,48,4096]{2,1,0:T(8,128)(2,1)}, u32[]{:S(2)}, u32[]{:S(2)}) %all-to-all-start.3) | async-done | bytes 3145760 | tf_op jit(solution)/shard_map/all_to_all | solution.py:88
  368.6 6.2 %gather_fusion.4 = bf16[256,4096]{1,0:T(8,128)(2,1)S(1)} fusion(bf16[384,4096]{1,0:T(8,128)(2,1)} %bitcast.14, s32[1024]{0:T(1024)S(1)} %pad_clamp_fusion.1), kind=kCustom, calls=%fused_computation.4 | custom fusion | bytes 4195328 | tf_op jit(solution)/shard_map/gather | solution.py:89
  374.8 2.9 gather.25
  377.7 7.9 %reduce_sum.35 = bf16[128,4096]{1,0:T(8,128)(2,1)} reduce(bf16[128,2,4096]{2,1,0:T(2,128)(2,1)} %gather.25, bf16[]{:T(256)} %constant.39.clone.1), dimensions={1}, to_apply=%region_5.6 | reduce | flops 524288 | bytes 3145730 | tf_op jit(solution)/shard_map/reduce_sum | solution.py:90
  385.6 9.6 %multiply_reduce_fusion = bf16[128,4096]{1,0:T(8,128)(2,1)} fusion(f32[128,2,4096]{2,1,0:T(2,128)} %reshape.118, f32[128,2]{1,0:T(8,128)S(1)} %copy.14), kind=kLoop, calls=%fused_computation.25 | loop fusion | flops 1572864 | bytes 5243904 | tf_op jit(solution)/shard_map/reduce_sum | solution.py:60
  395.2 2.6 copy.19
  (28 shorter events, 0.2 us)
Async XLA Ops:
  7.2 8.4 %copy-start = (bf16[128,4096]{1,0:T(8,128)(2,1)S(1)}, bf16[128,4096]{1,0:T(8,128)(2,1)}, u32[]{:S(2)}) copy-start(bf16[128,4096]{1,0:T(8,128)(2,1)} %param.13) | copy-start | bytes 3145732
  24.2 7.5 %copy-start.2 = (bf16[128,4096]{1,0:T(8,128)(2,1)S(1)}, bf16[128,4096]{1,0:T(8,128)(2,1)}, u32[]{:S(2)}) copy-start(bf16[128,4096]{1,0:T(8,128)(2,1)} %param.7) | copy-start | bytes 3145732
  24.2 78.2 %all-to-all-start.2 = ((bf16[8,48,4096]{2,1,0:T(8,128)(2,1)}), bf16[8,48,4096]{2,1,0:T(8,128)(2,1)}, u32[]{:S(2)}, u32[]{:S(2)}) async-start(bf16[8,48,4096]{2,1,0:T(8,128)(2,1)} %fusion), calls=%async_computation.2 | async-start | bytes 6291456 | tf_op jit(solution)/shard_map/all_to_all | solution.py:66
  102.4 74.5 %all-to-all-start = ((bf16[8,48,4096]{2,1,0:T(8,128)(2,1)}), bf16[8,48,4096]{2,1,0:T(8,128)(2,1)S(1)}, u32[]{:S(2)}, u32[]{:S(2)}) async-start(bf16[8,48,4096]{2,1,0:T(8,128)(2,1)} %broadcast_select_fusion), calls=%async_computation | async-start | bytes 6291456 | tf_op jit(solution)/shard_map/all_to_all | solution.py:40
  106.1 289.1 %reduce-scatter.8.cloned.1.call-start = ((), (), s32[]{:S(2)}) async-start(), calls=%async_computation.9 | async-start | bytes 7864320 | tf_op jit(solution)/shard_map/reduce_scatter | solution.py:114
  176.9 5.5 %copy-start.6 = (f32[384,768]{1,0:T(8,128)S(1)}, f32[384,768]{1,0:T(8,128)}, u32[]{:S(2)}) copy-start(f32[384,768]{1,0:T(8,128)} %fusion.1) | copy-start | bytes 3538948
  189.2 0.8 copy-start.4
  198.1 199.7 %reduce-scatter.4.cloned.1.call-start = ((), (), s32[]{:S(2)}) async-start(), calls=%async_computation.7 | async-start | bytes 7864320 | tf_op jit(solution)/shard_map/reduce_scatter | solution.py:95
  204.6 193.2 %reduce-scatter.6.cloned.1.call-start = ((), (), s32[]{:S(2)}) async-start(), calls=%async_computation.8 | async-start | bytes 7864320 | tf_op jit(solution)/shard_map/reduce_scatter | solution.py:104
  211.4 1.1 copy-start.5
  219.3 74.7 %all-to-all-start.1 = ((bf16[8,48,4096]{2,1,0:T(8,128)(2,1)}), bf16[8,48,4096]{2,1,0:T(8,128)(2,1)S(1)}, u32[]{:S(2)}, u32[]{:S(2)}) async-start(bf16[8,48,4096]{2,1,0:T(8,128)(2,1)} %bitcast.66), calls=%async_computation.1 | async-start | bytes 6291456 | tf_op jit(solution)/shard_map/all_to_all | solution.py:50
  223.0 5.0 %copy-start.3 = (bf16[384,768]{1,0:T(8,128)(2,1)S(1)}, bf16[384,768]{1,0:T(8,128)(2,1)}, u32[]{:S(2)}) copy-start(bf16[384,768]{1,0:T(8,128)(2,1)} %get-tuple-element.17) | copy-start | bytes 1769476
  294.0 74.6 %all-to-all-start.3 = ((bf16[8,48,4096]{2,1,0:T(8,128)(2,1)}), bf16[8,48,4096]{2,1,0:T(8,128)(2,1)}, u32[]{:S(2)}, u32[]{:S(2)}) async-start(bf16[8,48,4096]{2,1,0:T(8,128)(2,1)} %bitcast.65), calls=%async_computation.3 | async-start | bytes 6291456 | tf_op jit(solution)/shard_map/all_to_all | solution.py:88
  377.7 20.1 %copy-start.1 = (bf16[128,4096]{1,0:T(8,128)(2,1)S(1)}, bf16[128,4096]{1,0:T(8,128)(2,1)}, u32[]{:S(2)}) copy-start(bf16[128,4096]{1,0:T(8,128)(2,1)} %param.13) | copy-start | bytes 3145732
Sparse Core Ops, SparseCore 0:
  198.2 57.3 reduce-scatter.7
  258.9 58.3 reduce-scatter.3
  320.4 58.3 reduce-scatter.5
where the time goes:
time: 410 us; the launch traced here: 405 us
  waiting for transfers between devices  245 us (60%)
  matrix products  61 us (15%)
  local copies, waits for them, and re-layouts  36.4 us (9%)
  other arithmetic  28.2 us (7%)
  starting transfers between devices  20 us (5%)
  between operations  14.2 us (3%)
    all_to_all x1, waiting for transfers between devices, per_device(): lax.all_to_all(outbound, 'expert', split_axis=0, concat_axis=0, tiled=True)  63 us
    all_to_all x1, waiting for transfers between devices, per_device(): lax.all_to_all(pair_grad, 'expert', split_axis=0, concat_axis=0, tiled=True)  62.8 us
    all_to_all x1, waiting for transfers between devices, per_device(): lax.all_to_all(input_grad, 'expert', split_axis=0, concat_axis=0, tiled=T...  61.5 us
    all_to_all x1, waiting for transfers between devices, per_device(): lax.all_to_all(produced, 'expert', split_axis=0, concat_axis=0, tiled=True)  57.5 us
    reduce_sum x1, other arithmetic, per_device(): jnp.sum(weighted.reshape(tok_count, top_count, model_width), axis=1)  9.64 us
    gather x2, local copies, waits for them, and re-layouts, per_device(): returned_grad.reshape(-1, model_width)[targets].astype(jnp.float32)  9.04 us
    dot_general x1, matrix products, per_device(): lax.dot_general(gate_pre_grad, gate_matrix, contract, preferred_element_t...  8.54 us
  transfers between devices with their start and end apart: 7, of which 4 were waited for; matrix products, arithmetic and copies ran while one was open for 21% of the time, Pallas kernels for 0%

commit v1 on v0

--- a/solution.py
+++ b/solution.py
@@ -2,6 +2,29 @@
 import jax.numpy as jnp
 from jax import lax
 from jax.sharding import PartitionSpec as P
+
+
+def split_up(x, dim, count):
+    dims = x.shape
+    blocks = x.reshape(*dims[:dim], count, dims[dim] // count, *dims[dim + 1 :])
+    return jnp.moveaxis(blocks, dim, 0)
+
+
+def laid_out(blocks, dim):
+    shape = list(blocks.shape[1:])
+    shape[dim] *= blocks.shape[0]
+    return jnp.moveaxis(blocks, 0, dim).reshape(shape)
+
+
+def exchange_directly(array, axis, split_dim, concat_dim):
+    size, index = (lax.axis_size(axis), lax.axis_index(axis))
+    pieces = split_up(array, split_dim, size)
+    outs = [pieces[index]]
+    for step in range(1, size):
+        sent = pieces[(index + step) % size]
+        outs.append(lax.ppermute(sent, axis, [(i, (i + step) % size) for i in range(size)]))
+    pieces = jnp.stack(outs)[(index - jnp.arange(size)) % size]
+    return laid_out(pieces, concat_dim)
 
 
 def slot_targets(block_ids, experts, capacity):
@@ -85,7 +108,7 @@
         up_pre_grad, up_matrix, contract, preferred_element_type=jnp.float32
     )
     input_grad = input_grad.astype(jnp.bfloat16).reshape(experts, capacity, model_width)
-    returned_grad = lax.all_to_all(input_grad, "expert", split_axis=0, concat_axis=0, tiled=True)
+    returned_grad = exchange_directly(input_grad, "expert", 0, 0)
     pair_input = returned_grad.reshape(-1, model_width)[targets].astype(jnp.float32)
     tokens_grad = jnp.sum(pair_input.reshape(tok_count, top_count, model_width), axis=1).astype(
         jnp.bfloat16

time: 410 us -> 439 us (1.071)
  starting transfers between devices: 20 us -> 39.9 us
  local copies, waits for them, and re-layouts: 36.4 us -> 52.4 us
  waiting for transfers between devices: 245 us -> 237 us
    ppermute x0 -> x7, waiting for transfers between devices: none -> 112 us  [exchange_directly(): lax.ppermute(sent, axis, [(i, (i + step) % size) for i in range(size)])]
    all_to_all x1 -> x0, waiting for transfers between devices: 61.5 us -> none  [per_device(): lax.all_to_all(input_grad, 'expert', split_axis=0, concat_axis=0, tiled=T...]
    all_to_all x1, waiting for transfers between devices: 57.5 us -> 0.01 us  [per_device(): lax.all_to_all(produced, 'expert', split_axis=0, concat_axis=0, tiled=True)]
    ppermute x0 -> x7, starting transfers between devices: none -> 23.4 us  [exchange_directly(): lax.ppermute(sent, axis, [(i, (i + step) % size) for i in range(size)])]
    unnamed x16 -> x32, local copies, waits for them, and re-layouts: 5.24 us -> 10.8 us
    all_to_all x1 -> x0, starting transfers between devices: 4.45 us -> none  [per_device(): lax.all_to_all(input_grad, 'expert', split_axis=0, concat_axis=0, tiled=T...]
  transfers between devices with their start and end apart: 7 -> 13, of which waited for: 4 -> 5; matrix products, arithmetic and copies ran while one was open for 21% -> 23% of each run, Pallas kernels for 0% -> 0%
where the time goes in v1:
time: 439 us; the launch traced here: 431 us
  waiting for transfers between devices  237 us (54%)
  matrix products  58.7 us (13%)
  local copies, waits for them, and re-layouts  52.4 us (12%)
  starting transfers between devices  39.9 us (9%)
  other arithmetic  27.9 us (6%)
  between operations  14.3 us (3%)
    ppermute x7, waiting for transfers between devices, exchange_directly(): lax.ppermute(sent, axis, [(i, (i + step) % size) for i in range(size)])  112 us
    all_to_all x1, waiting for transfers between devices, per_device(): lax.all_to_all(outbound, 'expert', split_axis=0, concat_axis=0, tiled=True)  62.9 us
    all_to_all x1, waiting for transfers between devices, per_device(): lax.all_to_all(pair_grad, 'expert', split_axis=0, concat_axis=0, tiled=True)  62.8 us
    ppermute x7, starting transfers between devices, exchange_directly(): lax.ppermute(sent, axis, [(i, (i + step) % size) for i in range(size)])  23.4 us
    gather x2, local copies, waits for them, and re-layouts, per_device(): returned_grad.reshape(-1, model_width)[targets].astype(jnp.float32)  12.2 us
    unnamed x32, local copies, waits for them, and re-layouts  10.8 us
    reduce_sum x1, other arithmetic, per_device(): jnp.sum(weighted.reshape(tok_count, top_count, model_width), axis=1)  9.64 us
    dot_general x1, matrix products, per_device(): lax.dot_general(up_pre_grad, up_matrix, contract, preferred_element_type=...  8.97 us
  transfers between devices with their start and end apart: 13, of which 5 were waited for; matrix products, arithmetic and copies ran while one was open for 23% of the time, Pallas kernels for 0%

profile of v1, /device:TPU:0, one launch (start us, length us, event | category | flops | bytes accessed | tf_op | source)
XLA Modules:
  0.0 430.7 jit_solution(3980607539644316753)
XLA Ops:
  7.2 0.8 broadcast_multiply_fusion
  8.0 0.8 copy.16
  9.0 0.7 convert_multiply_fusion.1
  11.2 1.4 scatter_custom_fusion
  12.6 2.8 gather_fusion.2
  15.5 4.1 gather_fusion.3
  19.6 4.5 %fusion = bf16[8,48,4096]{2,1,0:T(8,128)(2,1)} fusion(bf16[8,48,4096]{2,1,0:T(8,128)(2,1)} %bitcast.92, f32[8,48]{1,0:T(8,128)S(1)} %mul.69), kind=kLoop, calls=%fused_computation.11 | loop fusion | flops 4718592 | bytes 6292992 | tf_op jit(solution)/shard_map/convert_element_type | solution.py:87
  24.1 7.4 %all-to-all-start.2 = ((bf16[8,48,4096]{2,1,0:T(8,128)(2,1)}), bf16[8,48,4096]{2,1,0:T(8,128)(2,1)}, u32[]{:S(2)}, u32[]{:S(2)}) async-start(bf16[8,48,4096]{2,1,0:T(8,128)(2,1)} %fusion), calls=%async_computation.2 | async-start | bytes 6291456 | tf_op jit(solution)/shard_map/all_to_all | solution.py:89
  31.6 4.1 gather_fusion
  35.7 3.8 broadcast_select_fusion
  39.5 62.8 %all-to-all-done.2 = bf16[8,48,4096]{2,1,0:T(8,128)(2,1)} async-done(((bf16[8,48,4096]{2,1,0:T(8,128)(2,1)}), bf16[8,48,4096]{2,1,0:T(8,128)(2,1)}, u32[]{:S(2)}, u32[]{:S(2)}) %all-to-all-start.2) | async-done | bytes 3145760 | tf_op jit(solution)/shard_map/all_to_all | solution.py:89
  102.4 3.6 all-to-all-start
  106.6 7.4 %fusion.1 = f32[384,768]{1,0:T(8,128)} fusion(bf16[384,4096]{1,0:T(8,128)(2,1)} %bitcast.12, bf16[1,768,4096]{2,1,0:T(8,128)(2,1)} %param.12), kind=kOutput, calls=%fused_computation.12 | convolution fusion | flops 2415919104 | bytes 10616832 | tf_op jit(solution)/shard_map/dot_general | solution.py:97
  114.0 62.9 %all-to-all-done = bf16[8,48,4096]{2,1,0:T(8,128)(2,1)S(1)} async-done(((bf16[8,48,4096]{2,1,0:T(8,128)(2,1)}), bf16[8,48,4096]{2,1,0:T(8,128)(2,1)S(1)}, u32[]{:S(2)}, u32[]{:S(2)}) %all-to-all-start) | async-done | bytes 3145760 | tf_op jit(solution)/shard_map/all_to_all | solution.py:63
  176.9 5.5 %fusion.7 = f32[384,768]{1,0:T(8,128)S(1)} fusion(bf16[384,4096]{1,0:T(8,128)(2,1)S(1)} %bitcast.95, bf16[1,4096,768]{2,1,0:T(8,128)(2,1)} %param.11), kind=kOutput, calls=%fused_computation.18 | convolution fusion | flops 2415919104 | bytes 10616832 | tf_op jit(solution)/shard_map/dot_general | solution.py:67
  182.4 6.8 %multiply_convert_fusion.1 = (bf16[384,768]{1,0:T(8,128)(2,1)}, bf16[384,768]{1,0:T(8,128)(2,1)}, bf16[384,768]{1,0:T(8,128)(2,1)S(1)}) fusion(f32[384,768]{1,0:T(8,128)S(1)} %copy-done.7, f32[384,768]{1,0:T(8,128)S(1)} %fusion.7, bf16[384,4096]{1,0:T(8,128)(2,1)S(1)} %bitcast.96, bf16[1,4096,768]{2,1,0:T(8,128)(2,1)} %param.10), kind=kOutput, calls=%fused_computation.29 | convolution fusion | flops 2420342784 | bytes 13565952 | tf_op jit(solution)/shard_map/dot_general | solution.py:66
  189.2 0.8 copy-done.4
  190.0 8.0 %convolution_convert_fusion = bf16[4096,768]{1,0:T(8,128)(2,1)} fusion(bf16[384,4096]{1,0:T(8,128)(2,1)} %bitcast.12, bf16[384,768]{1,0:T(8,128)(2,1)S(1)} %get-tuple-element.27), kind=kOutput, calls=%fused_computation.7 | convolution fusion | flops 2419064832 | bytes 10027008 | tf_op jit(solution)/shard_map/dot_general | solution.py:138
  198.1 6.4 %convolution_convert_fusion.2 = bf16[4096,768]{1,0:T(8,128)(2,1)} fusion(bf16[384,4096]{1,0:T(8,128)(2,1)S(1)} %bitcast.97, bf16[384,768]{1,0:T(8,128)(2,1)} %get-tuple-element.25), kind=kOutput, calls=%fused_computation.9 | convolution fusion | flops 2419064832 | bytes 10027008 | tf_op jit(solution)/shard_map/dot_general | solution.py:119
  204.7 6.6 %convolution_convert_fusion.1 = bf16[4096,768]{1,0:T(8,128)(2,1)} fusion(bf16[384,4096]{1,0:T(8,128)(2,1)S(1)} %bitcast.98, bf16[384,768]{1,0:T(8,128)(2,1)} %get-tuple-element.26), kind=kOutput, calls=%fused_computation.8 | convolution fusion | flops 2419064832 | bytes 10027008 | tf_op jit(solution)/shard_map/dot_general | solution.py:128
  211.6 0.9 copy-done.3
  212.4 9.0 %fusion.5 = f32[384,4096]{1,0:T(8,128)} fusion(bf16[384,768]{1,0:T(8,128)(2,1)S(1)} %copy-done.3, bf16[1,4096,768]{2,1,0:T(8,128)(2,1)} %param.11), kind=kOutput, calls=%fused_computation.16 | convolution fusion | flops 2415919104 | bytes 13172736 | tf_op jit(solution)/shard_map/dot_general | solution.py:107
  221.5 5.0 %add_convert_fusion = bf16[384,4096]{1,0:T(8,128)(2,1)S(1)} fusion(f32[384,4096]{1,0:T(8,128)} %fusion.5, bf16[384,768]{1,0:T(8,128)(2,1)S(1)} %copy-done.6, bf16[1,4096,768]{2,1,0:T(8,128)(2,1)S(1)} %bitcast.105), kind=kOutput, calls=%fused_computation.24 | convolution fusion | flops 2419064832 | bytes 16318464 | tf_op jit(solution)/shard_map/dot_general | solution.py:104
  226.4 1.7 dynamic-slice_bitcast_fusion
  228.2 1.3 collective-permute-start
  229.5 4.0 fusion.15
  233.5 4.7 %all-to-all-start.1 = ((bf16[8,48,4096]{2,1,0:T(8,128)(2,1)}), bf16[8,48,4096]{2,1,0:T(8,128)(2,1)S(1)}, u32[]{:S(2)}, u32[]{:S(2)}) async-start(bf16[8,48,4096]{2,1,0:T(8,128)(2,1)} %bitcast.94), calls=%async_computation.1 | async-start | bytes 6291456 | tf_op jit(solution)/shard_map/all_to_all | solution.py:73
  238.2 4.7 %collective-permute-start.6 = (bf16[1,48,4096]{2,1,0:T(8,128)(2,1)}, bf16[1,48,4096]{2,1,0:T(8,128)(2,1)S(1)}, u32[]{:S(2)}, u32[]{:S(2)}) collective-permute-start(bf16[1,48,4096]{2,1,0:T(8,128)(2,1)} %get-tuple-element.17), channel_id=1, source_target_pairs={{0,7},{1,0},{2,1},{3,2},{4,3},{5,4},{6,5},{7,6},{8,15},{9,8},{10,9... | collective-permute-start | bytes 1179656 | tf_op jit(solution)/shard_map/ppermute | solution.py:25
  243.5 2.9 collective-permute-start.3
  246.4 1.8 bitcast_dynamic-update-slice_fusion.6
  248.2 87.6 %collective-permute-done.1 = bf16[1,48,4096]{2,1,0:T(8,128)(2,1)S(1)} collective-permute-done((bf16[1,48,4096]{2,1,0:T(8,128)(2,1)}, bf16[1,48,4096]{2,1,0:T(8,128)(2,1)S(1)}, u32[]{:S(2)}, u32[]{:S(2)}) %collective-permute-start.1) | collective-permute-done | bytes 393248 | tf_op jit(solution)/shard_map/ppermute | solution.py:25
  335.8 13.8 %collective-permute-start.2 = (bf16[1,48,4096]{2,1,0:T(8,128)(2,1)}, bf16[1,48,4096]{2,1,0:T(8,128)(2,1)S(1)}, u32[]{:S(2)}, u32[]{:S(2)}) collective-permute-start(bf16[1,48,4096]{2,1,0:T(8,128)(2,1)} %get-tuple-element.21), channel_id=1, source_target_pairs={{0,3},{1,4},{2,5},{3,6},{4,7},{5,0},{6,1},{7,2},{8,11},{9,12},{10,... | collective-permute-start | bytes 1179656 | tf_op jit(solution)/shard_map/ppermute | solution.py:25
  349.7 0.8 bitcast_dynamic-update-slice_fusion.5
  350.5 10.6 %collective-permute-done.2 = bf16[1,48,4096]{2,1,0:T(8,128)(2,1)S(1)} collective-permute-done((bf16[1,48,4096]{2,1,0:T(8,128)(2,1)}, bf16[1,48,4096]{2,1,0:T(8,128)(2,1)S(1)}, u32[]{:S(2)}, u32[]{:S(2)}) %collective-permute-start.2) | collective-permute-done | bytes 393248 | tf_op jit(solution)/shard_map/ppermute | solution.py:25
  361.1 0.8 bitcast_dynamic-update-slice_fusion.4
  361.9 13.4 %collective-permute-done.3 = bf16[1,48,4096]{2,1,0:T(8,128)(2,1)S(1)} collective-permute-done((bf16[1,48,4096]{2,1,0:T(8,128)(2,1)}, bf16[1,48,4096]{2,1,0:T(8,128)(2,1)S(1)}, u32[]{:S(2)}, u32[]{:S(2)}) %collective-permute-start.3) | collective-permute-done | bytes 393248 | tf_op jit(solution)/shard_map/ppermute | solution.py:25
  375.3 0.8 bitcast_dynamic-update-slice_fusion.3
  376.1 0.8 bitcast_dynamic-update-slice_fusion.2
  376.8 0.8 bitcast_dynamic-update-slice_fusion.1
  377.6 0.8 bitcast_dynamic-update-slice_fusion
  378.4 4.4 %gather_fusion.4 = bf16[8,48,4096]{2,1,0:T(8,128)(2,1)} fusion(bf16[8,48,4096]{2,1,0:T(8,128)(2,1)} %bitcast.93, s32[1024]{0:T(1024)S(1)} %pad_clamp_fusion), kind=kCustom, calls=%fused_computation.4 | custom fusion | bytes 6291488 | tf_op jit(solution)/shard_map/gather | solution.py:26
  382.8 7.5 %gather_fusion.5 = bf16[256,4096]{1,0:T(8,128)(2,1)} fusion(bf16[384,4096]{1,0:T(8,128)(2,1)} %bitcast.90, s32[1024]{0:T(1024)S(1)} %pad_clamp_fusion.2), kind=kCustom, calls=%fused_computation.5 | custom fusion | bytes 4195328 | tf_op jit(solution)/shard_map/gather | solution.py:112
  390.4 4.6 %gather.29 = bf16[128,2,4096]{2,1,0:T(2,128)(2,1)} reshape(bf16[256,4096]{1,0:T(8,128)(2,1)} %gather_fusion.5) | data formatting | bytes 4194304 | tf_op jit(solution)/shard_map/gather | solution.py:112
  395.0 7.7 %reduce_sum.35 = bf16[128,4096]{1,0:T(8,128)(2,1)} reduce(bf16[128,2,4096]{2,1,0:T(2,128)(2,1)} %gather.29, bf16[]{:T(256)} %constant.92.clone.1), dimensions={1}, to_apply=%region_5.6 | reduce | flops 524288 | bytes 3145730 | tf_op jit(solution)/shard_map/reduce_sum | solution.py:113
  402.7 3.2 gather_fusion.1
  405.9 5.8 %reshape.159 = f32[128,2,4096]{2,1,0:T(2,128)} reshape(bf16[256,4096]{1,0:T(8,128)(2,1)} %gather_fusion.1) | data formatting | bytes 6291456 | tf_op jit(solution)/shard_map/convert_element_type | solution.py:81
  411.7 9.6 %multiply_reduce_fusion = bf16[128,4096]{1,0:T(8,128)(2,1)} fusion(f32[128,2,4096]{2,1,0:T(2,128)} %reshape.159, f32[128,2]{1,0:T(8,128)S(1)} %copy.14), kind=kLoop, calls=%fused_computation.26 | loop fusion | flops 1572864 | bytes 5243904 | tf_op jit(solution)/shard_map/reduce_sum | solution.py:83
  421.3 2.6 copy.19
  (63 shorter events, 3.4 us)
Async XLA Ops:
  7.2 8.4 %copy-start = (bf16[128,4096]{1,0:T(8,128)(2,1)S(1)}, bf16[128,4096]{1,0:T(8,128)(2,1)}, u32[]{:S(2)}) copy-start(bf16[128,4096]{1,0:T(8,128)(2,1)} %param.13) | copy-start | bytes 3145732
  24.1 7.5 %copy-start.2 = (bf16[128,4096]{1,0:T(8,128)(2,1)S(1)}, bf16[128,4096]{1,0:T(8,128)(2,1)}, u32[]{:S(2)}) copy-start(bf16[128,4096]{1,0:T(8,128)(2,1)} %param.7) | copy-start | bytes 3145732
  24.1 78.2 %all-to-all-start.2 = ((bf16[8,48,4096]{2,1,0:T(8,128)(2,1)}), bf16[8,48,4096]{2,1,0:T(8,128)(2,1)}, u32[]{:S(2)}, u32[]{:S(2)}) async-start(bf16[8,48,4096]{2,1,0:T(8,128)(2,1)} %fusion), calls=%async_computation.2 | async-start | bytes 6291456 | tf_op jit(solution)/shard_map/all_to_all | solution.py:89
  102.4 74.5 %all-to-all-start = ((bf16[8,48,4096]{2,1,0:T(8,128)(2,1)}), bf16[8,48,4096]{2,1,0:T(8,128)(2,1)S(1)}, u32[]{:S(2)}, u32[]{:S(2)}) async-start(bf16[8,48,4096]{2,1,0:T(8,128)(2,1)} %broadcast_select_fusion), calls=%async_computation | async-start | bytes 6291456 | tf_op jit(solution)/shard_map/all_to_all | solution.py:63
  106.0 315.3 %reduce-scatter.8.cloned.1.call-start = ((), (), s32[]{:S(2)}) async-start(), calls=%async_computation.8 | async-start | bytes 7864320 | tf_op jit(solution)/shard_map/reduce_scatter | solution.py:137
  176.9 5.5 %copy-start.7 = (f32[384,768]{1,0:T(8,128)S(1)}, f32[384,768]{1,0:T(8,128)}, u32[]{:S(2)}) copy-start(f32[384,768]{1,0:T(8,128)} %fusion.1) | copy-start | bytes 3538948
  189.2 0.8 copy-start.4
  198.0 225.9 %reduce-scatter.4.cloned.1.call-start = ((), (), s32[]{:S(2)}) async-start(), calls=%async_computation.6 | async-start | bytes 7864320 | tf_op jit(solution)/shard_map/reduce_scatter | solution.py:118
  204.5 219.4 %reduce-scatter.6.cloned.1.call-start = ((), (), s32[]{:S(2)}) async-start(), calls=%async_computation.7 | async-start | bytes 7864320 | tf_op jit(solution)/shard_map/reduce_scatter | solution.py:127
  211.4 1.1 copy-start.3
  211.4 10.0 %slice-start = ((s8[6291456]{0:T(1024)(128)(4,1)}), s8[2097152]{0:T(1024)(128)(4,1)S(1)}, s32[]{:S(2)}) async-start(s8[6291456]{0:T(1024)(128)(4,1)} %bitcast.104), calls=%async_computation.9 | async-start | bytes 4194304
  212.4 9.0 %slice-start.1 = ((s8[6291456]{0:T(1024)(128)(4,1)}), s8[4194304]{0:T(1024)(128)(4,1)S(1)}, s32[]{:S(2)}) async-start(s8[6291456]{0:T(1024)(128)(4,1)} %bitcast.104), calls=%async_computation.10 | async-start | bytes 8388608
  212.4 9.0 %copy-start.6 = (bf16[384,768]{1,0:T(8,128)(2,1)S(1)}, bf16[384,768]{1,0:T(8,128)(2,1)}, u32[]{:S(2)}) copy-start(bf16[384,768]{1,0:T(8,128)(2,1)} %get-tuple-element.25) | copy-start | bytes 1769476
  212.4 17.0 %slice-start.2 = ((s8[6291456]{0:T(1024)(128)(4,1)}), s8[4194304]{0:T(1024)(128)(4,1)S(1)}, s32[]{:S(2)}) async-start(s8[6291456]{0:T(1024)(128)(4,1)} %bitcast.106), calls=%async_computation.11 | async-start | bytes 8388608
  221.4 8.1 %slice-start.3 = ((s8[6291456]{0:T(1024)(128)(4,1)}), s8[2097152]{0:T(1024)(128)(4,1)S(1)}, s32[]{:S(2)}) async-start(s8[6291456]{0:T(1024)(128)(4,1)} %bitcast.106), calls=%async_computation.12 | async-start | bytes 4194304
  226.4 3.1 copy-start.5
  228.2 18.3 %collective-permute-start = (bf16[1,48,4096]{2,1,0:T(8,128)(2,1)}, bf16[1,48,4096]{2,1,0:T(8,128)(2,1)}, u32[]{:S(2)}, u32[]{:S(2)}) collective-permute-start(bf16[1,48,4096]{2,1,0:T(8,128)(2,1)} %get-tuple-element.23), channel_id=1, source_target_pairs={{0,1},{1,2},{2,3},{3,4},{4,5},{5,6},{6,7},{7,0},{8,9},{9,10},{10,1... | collective-permute-start | bytes 1179656 | tf_op jit(solution)/shard_map/ppermute | solution.py:25
  233.5 169.1 %all-to-all-start.1 = ((bf16[8,48,4096]{2,1,0:T(8,128)(2,1)}), bf16[8,48,4096]{2,1,0:T(8,128)(2,1)S(1)}, u32[]{:S(2)}, u32[]{:S(2)}) async-start(bf16[8,48,4096]{2,1,0:T(8,128)(2,1)} %bitcast.94), calls=%async_computation.1 | async-start | bytes 6291456 | tf_op jit(solution)/shard_map/all_to_all | solution.py:73
  238.2 139.4 %collective-permute-start.6 = (bf16[1,48,4096]{2,1,0:T(8,128)(2,1)}, bf16[1,48,4096]{2,1,0:T(8,128)(2,1)S(1)}, u32[]{:S(2)}, u32[]{:S(2)}) collective-permute-start(bf16[1,48,4096]{2,1,0:T(8,128)(2,1)} %get-tuple-element.17), channel_id=1, source_target_pairs={{0,7},{1,0},{2,1},{3,2},{4,3},{5,4},{6,5},{7,6},{8,15},{9,8},{10,9... | collective-permute-start | bytes 1179656 | tf_op jit(solution)/shard_map/ppermute | solution.py:25
  242.9 133.9 %collective-permute-start.5 = (bf16[1,48,4096]{2,1,0:T(8,128)(2,1)}, bf16[1,48,4096]{2,1,0:T(8,128)(2,1)S(1)}, u32[]{:S(2)}, u32[]{:S(2)}) collective-permute-start(bf16[1,48,4096]{2,1,0:T(8,128)(2,1)} %get-tuple-element.18), channel_id=1, source_target_pairs={{0,6},{1,7},{2,0},{3,1},{4,2},{5,3},{6,4},{7,5},{8,14},{9,15},{10,... | collective-permute-start | bytes 1179656 | tf_op jit(solution)/shard_map/ppermute | solution.py:25
  243.5 132.6 %collective-permute-start.4 = (bf16[1,48,4096]{2,1,0:T(8,128)(2,1)}, bf16[1,48,4096]{2,1,0:T(8,128)(2,1)S(1)}, u32[]{:S(2)}, u32[]{:S(2)}) collective-permute-start(bf16[1,48,4096]{2,1,0:T(8,128)(2,1)} %get-tuple-element.19), channel_id=1, source_target_pairs={{0,5},{1,6},{2,7},{3,0},{4,1},{5,2},{6,3},{7,4},{8,13},{9,14},{10,... | collective-permute-start | bytes 1179656 | tf_op jit(solution)/shard_map/ppermute | solution.py:25
  243.5 131.8 %collective-permute-start.3 = (bf16[1,48,4096]{2,1,0:T(8,128)(2,1)}, bf16[1,48,4096]{2,1,0:T(8,128)(2,1)S(1)}, u32[]{:S(2)}, u32[]{:S(2)}) collective-permute-start(bf16[1,48,4096]{2,1,0:T(8,128)(2,1)} %get-tuple-element.20), channel_id=1, source_target_pairs={{0,4},{1,5},{2,6},{3,7},{4,0},{5,1},{6,2},{7,3},{8,12},{9,13},{10,... | collective-permute-start | bytes 1179656 | tf_op jit(solution)/shard_map/ppermute | solution.py:25
  246.4 89.4 %collective-permute-start.1 = (bf16[1,48,4096]{2,1,0:T(8,128)(2,1)}, bf16[1,48,4096]{2,1,0:T(8,128)(2,1)S(1)}, u32[]{:S(2)}, u32[]{:S(2)}) collective-permute-start(bf16[1,48,4096]{2,1,0:T(8,128)(2,1)} %get-tuple-element.22), channel_id=1, source_target_pairs={{0,2},{1,3},{2,4},{3,5},{4,6},{5,7},{6,0},{7,1},{8,10},{9,11},{10,... | collective-permute-start | bytes 1179656 | tf_op jit(solution)/shard_map/ppermute | solution.py:25
  335.8 25.3 %collective-permute-start.2 = (bf16[1,48,4096]{2,1,0:T(8,128)(2,1)}, bf16[1,48,4096]{2,1,0:T(8,128)(2,1)S(1)}, u32[]{:S(2)}, u32[]{:S(2)}) collective-permute-start(bf16[1,48,4096]{2,1,0:T(8,128)(2,1)} %get-tuple-element.21), channel_id=1, source_target_pairs={{0,3},{1,4},{2,5},{3,6},{4,7},{5,0},{6,1},{7,2},{8,11},{9,12},{10,... | collective-permute-start | bytes 1179656 | tf_op jit(solution)/shard_map/ppermute | solution.py:25
  405.9 18.0 %copy-start.1 = (bf16[128,4096]{1,0:T(8,128)(2,1)S(1)}, bf16[128,4096]{1,0:T(8,128)(2,1)}, u32[]{:S(2)}) copy-start(bf16[128,4096]{1,0:T(8,128)(2,1)} %param.13) | copy-start | bytes 3145732
Sparse Core Ops, SparseCore 0:
  198.1 57.4 reduce-scatter.7
  258.9 58.3 reduce-scatter.3
  320.4 58.3 reduce-scatter.5
